TPU v7x, 32 devices: a whole 2x2x4 slice. The times are simulated.
32 devices in a mesh: groups: 2 (over y), seq: 4 (over z), section: 2 (over x), chan: 2 (over core).
Axes of the slice: x: 2, y: 2, z: 4, core: 2. Of those that a mesh axis runs over, the one named last changes fastest.
Arguments:
- base_codes: int32 [131072], P(('groups', 'seq', 'section')), parts along dimension 0, may hold values from 0 to 3
- stem_weight: bfloat16 [64, 768], replicated, as said below
- conv_gain: float32 [768], replicated, may hold values from 0.1 to 1.9
- dilated_conv_weight: bfloat16 [3, 768, 768], P(None, None, 'chan'), may hold values from -0.125 to 0.125
- widen_weight: bfloat16 [768, 1536], P(None, 'chan'), may hold values from -0.21875 to 0.21875
- token_gain: float32 [1536], replicated, may hold values from 0.1 to 1.9
- proj_weight: bfloat16 [1536, 256], replicated, may hold values from -0.15625 to 0.15625
- dist_weight: float32 [128], replicated, may hold values from -4 to 4
- pair_weight_one: bfloat16 [3, 3, 128, 128], P(None, None, None, 'chan'), may hold values from -0.1875 to 0.1875
- pair_weight_two: bfloat16 [3, 3, 128, 128], P(None, None, None, 'chan'), may hold values from -0.1875 to 0.1875
Outputs:
- fine_features: bfloat16 [4096, 1536], P(('groups', 'seq', 'section'), 'chan'), parts along dimension 0
- pair_map: bfloat16 [128, 64, 32], P('chan', ('groups', 'seq'), 'section'), parts along dimension 1
There are 2 independent parts, one for each index of `groups`. A program takes and returns all parts, laid end to end along the dimension named above; an argument that names none is the same for every part. Nothing has to cross between parts.
Inputs may be any that keep to these rules, and one draw needn't show every extreme that they name: Each entry of stem_weight is under 9 / sqrt(16) in magnitude.
All inputs are finite; a program needn't handle non-finite values.
Results may differ from a plain program's by a relative error of at most 0.015.
Values may be sent and summed in bfloat16 or wider, within the bound.
No kernel may reach another device: no remote copies, remote signals or barrier semaphores. Data moves between devices by JAX's collectives and lax.ppermute only.
A program may use at most 64 MiB of HBM per device.

v0:
```python
import math
import jax
import jax.numpy as jnp
from jax import lax
from jax.sharding import PartitionSpec as P

PC = 128
PATCH = 16
POOL = 64
DILATION_ROWS = 4
epsilon = 1e-06


def padded(cells, sides, width):
    for axis, dim in sides:
        count = lax.axis_size(axis)
        ends = count - 1
        head = lax.slice_in_dim(cells, 0, width, axis=dim)
        tail = lax.slice_in_dim(cells, cells.shape[dim] - width, cells.shape[dim], axis=dim)
        cells = jnp.concatenate(
            [
                lax.ppermute(tail, axis, [(i, (i + 1) % count) for i in range(ends)]),
                cells,
                lax.ppermute(head, axis, [((i + 1) % count, i) for i in range(ends)]),
            ],
            axis=dim,
        )
    return cells


def row_norm(values, gain):
    mean_square = jnp.mean(values * values, axis=1, keepdims=True)
    return values * lax.rsqrt(mean_square + epsilon) * gain


def pair_conv(active, weight):
    row_len = active.shape[1] - 2
    col_len = active.shape[2] - 2
    total = jnp.zeros((weight.shape[3], row_len, col_len), jnp.float32)
    for shift_row in range(3):
        for shift_col in range(3):
            window = active[:, shift_row : shift_row + row_len, shift_col : shift_col + col_len]
            total = total + jnp.einsum(
                "co,crs->ors",
                weight[shift_row, shift_col],
                window,
                preferred_element_type=jnp.float32,
            )
    return total


def make_pair(row_factor, col_factor, row_index, col_index, dist_weight, tokens_total):
    gap = jnp.abs(row_index[:, None] - col_index[None, :]).astype(jnp.float32)
    distance = jnp.log1p(gap) / math.log(tokens_total)
    product = (
        row_factor.astype(jnp.float32).T[:, :, None] * col_factor.astype(jnp.float32).T[:, None, :]
    )
    return product + dist_weight[:, None, None] * distance[None, :, :]


def per_device(
    base_codes,
    stem_weight,
    conv_gain,
    dilated_conv_weight,
    widen_weight,
    token_gain,
    proj_weight,
    dist_weight,
    pair_weight_one,
    pair_weight_two,
):
    count_of_rows = base_codes.shape[0] // PATCH
    coded = base_codes.reshape(count_of_rows, PATCH)
    onehot = (
        (coded[:, :, None] == jnp.arange(4, dtype=jnp.int32)[None, None, :])
        .astype(jnp.bfloat16)
        .reshape(count_of_rows, 4 * PATCH)
    )
    half_width = dilated_conv_weight.shape[2]
    own_index = lax.axis_index("chan")
    weight_own = lax.dynamic_slice_in_dim(stem_weight, own_index * half_width, half_width, 1)
    stem_own = jnp.dot(onehot, weight_own, preferred_element_type=jnp.float32).astype(jnp.bfloat16)
    full_stem_output = lax.all_gather(stem_own, "chan", axis=1, tiled=True)
    padded_rows = padded(full_stem_output, ((("seq", "section"), 0),), DILATION_ROWS)
    normalized_rows = row_norm(padded_rows.astype(jnp.float32), conv_gain).astype(jnp.bfloat16)
    summed_taps = jnp.zeros((count_of_rows, half_width), jnp.float32)
    for row_shift_amount in range(3):
        summed_taps = summed_taps + jnp.dot(
            normalized_rows[
                row_shift_amount * DILATION_ROWS : row_shift_amount * DILATION_ROWS + count_of_rows
            ],
            dilated_conv_weight[row_shift_amount],
            preferred_element_type=jnp.float32,
        )
    tower = (stem_own.astype(jnp.float32) + jax.nn.gelu(summed_taps)).astype(jnp.bfloat16)
    halved = jnp.maximum(tower[0::2], tower[1::2])
    widened = jnp.dot(
        lax.all_gather(halved, "chan", axis=1, tiled=True),
        widen_weight,
        preferred_element_type=jnp.float32,
    )
    fine_features = jax.nn.gelu(widened).astype(jnp.bfloat16)
    tok_count = fine_features.shape[0] // POOL
    token = jnp.mean(
        fine_features.astype(jnp.float32).reshape(tok_count, POOL, fine_features.shape[1]), axis=1
    ).astype(jnp.bfloat16)
    token_full = lax.all_gather(token, "chan", axis=1, tiled=True)
    token_norm = row_norm(token_full.astype(jnp.float32), token_gain).astype(jnp.bfloat16)
    factors = jnp.dot(token_norm, proj_weight, preferred_element_type=jnp.float32).astype(
        jnp.bfloat16
    )
    seq_count = lax.axis_size("seq")
    section_count = lax.axis_size("section")
    tokens_total = tok_count * seq_count * section_count
    tile_height = tok_count * section_count
    tile_width = tok_count * seq_count
    row_anchor = lax.axis_index("seq") * tile_height
    col_anchor = lax.axis_index("section") * tile_width
    pair_own = pair_weight_one.shape[3]
    every_token = lax.all_gather(factors, ("seq", "section"), axis=0, tiled=True)
    zero_padded = jnp.pad(every_token, ((1, 1), (0, 0)))
    row_factor = lax.dynamic_slice_in_dim(zero_padded, row_anchor, tile_height + 2, 0)[:, :PC]
    col_factor = lax.dynamic_slice_in_dim(zero_padded, col_anchor, tile_width + 2, 0)[:, PC:]
    row_index = row_anchor - 1 + jnp.arange(tile_height + 2, dtype=jnp.int32)
    col_index = col_anchor - 1 + jnp.arange(tile_width + 2, dtype=jnp.int32)
    extended = make_pair(
        row_factor, col_factor, row_index, col_index, dist_weight, tokens_total
    ).astype(jnp.bfloat16)
    row_valid = (row_index >= 0) & (row_index < tokens_total)
    col_valid = (col_index >= 0) & (col_index < tokens_total)
    inside = row_valid[:, None] & col_valid[None, :]
    act_one = jnp.where(inside[None, :, :], jax.nn.gelu(extended.astype(jnp.float32)), 0.0).astype(
        jnp.bfloat16
    )
    pair_start = extended[:, 1:-1, 1:-1]
    start_own = lax.dynamic_slice_in_dim(pair_start, own_index * pair_own, pair_own, 0)
    pair_mid = (start_own.astype(jnp.float32) + pair_conv(act_one, pair_weight_one)).astype(
        jnp.bfloat16
    )
    mid_full = lax.all_gather(pair_mid, "chan", axis=0, tiled=True)
    act_local_two = jax.nn.gelu(mid_full.astype(jnp.float32)).astype(jnp.bfloat16)
    act_two = padded(act_local_two, (("seq", 1), ("section", 2)), 1)
    pair_map = (pair_mid.astype(jnp.float32) + pair_conv(act_two, pair_weight_two)).astype(
        jnp.bfloat16
    )
    return (fine_features, pair_map)


def solution(mesh):
    in_specs = (
        P(("groups", "seq", "section")),
        P(),
        P(),
        P(None, None, "chan"),
        P(None, "chan"),
        P(),
        P(),
        P(),
        P(None, None, None, "chan"),
        P(None, None, None, "chan"),
    )
    out_specs = (P(("groups", "seq", "section"), "chan"), P("chan", ("groups", "seq"), "section"))
    return jax.shard_map(
        per_device, mesh=mesh, in_specs=in_specs, out_specs=out_specs, check_vma=False
    )
```

profile of v0, /device:TPU:0, one launch (start us, length us, event | category | flops | bytes accessed | tf_op | source)
XLA Modules:
  0.0 73.8 jit_solution(9603304205572424095)
XLA Ops:
  0.7 1.0 %eq.22 = s32[512,16]{1,0:T(8,128)S(1)} reshape(s32[8192]{0:T(1024)} %param.10) | data formatting | bytes 65536 | tf_op jit(solution)/shard_map/eq | solution.py:76
  1.9 1.2 %convolution_convert_fusion = bf16[512,384]{1,0:T(8,128)(2,1)S(1)} fusion(s32[512,64]{0,1:T(8,128)S(1)} %eq.24, s32[64]{0:T(128)S(1)} %eq.26, bf16[64,768]{1,0:T(8,128)(2,1)} %param.11, s32[]{:T(128)S(6)} %select_n.16), kind=kOutput, calls=%fused_computation.7 | convolution fusion | flops 25395200 | bytes 573700 | tf_op jit(solution)/shard_map/dot_general | solution.py:83
  3.1 2.5 %all_gather.15 = bf16[512,768]{1,0:T(8,128)(2,1)S(1)} all-gather(bf16[512,384]{1,0:T(8,128)(2,1)S(1)} %convolution_convert_fusion), channel_id=1, replica_groups=mesh['groups'=2,'seq'=4,'section'=2,'chan'=2] {'chan'}, dimensions={1}, use_global_device_ids=true | all-gather | bytes 1179648 | tf_op jit(solution)/shard_map/all_gather | solution.py:84
  5.6 4.8 %collective-permute-start = (bf16[4,768]{1,0:T(4,128)(2,1)S(1)}, bf16[4,768]{1,0:T(4,128)(2,1)S(1)}, u32[]{:S(2)}, u32[]{:S(2)}) collective-permute-start(bf16[4,768]{1,0:T(4,128)(2,1)S(1)} %get-tuple-element.4), channel_id=1, source_target_pairs={{0,2},{2,4},{4,6},{6,8},{8,10},{10,12},{12,14},{1,3},{3,5},{5,7},{... | collective-permute-start | bytes 18440 | tf_op jit(solution)/shard_map/ppermute | solution.py:22
  10.4 1.3 %collective-permute-start.1 = (bf16[4,768]{1,0:T(4,128)(2,1)S(1)}, bf16[4,768]{1,0:T(4,128)(2,1)S(1)}, u32[]{:S(2)}, u32[]{:S(2)}) collective-permute-start(bf16[4,768]{1,0:T(4,128)(2,1)S(1)} %get-tuple-element.5), channel_id=1, source_target_pairs={{2,0},{4,2},{6,4},{8,6},{10,8},{12,10},{14,12},{3,1},{5,3},{7,5},{... | collective-permute-start | bytes 18440 | tf_op jit(solution)/shard_map/ppermute | solution.py:24
  11.9 4.0 %collective-permute-done.1 = bf16[4,768]{1,0:T(4,128)(2,1)S(1)} collective-permute-done((bf16[4,768]{1,0:T(4,128)(2,1)S(1)}, bf16[4,768]{1,0:T(4,128)(2,1)S(1)}, u32[]{:S(2)}, u32[]{:S(2)}) %collective-permute-start.1) | collective-permute-done | bytes 6176 | tf_op jit(solution)/shard_map/ppermute | solution.py:24
  15.9 0.3 fusion
  16.3 0.3 fusion.2
  16.6 0.6 fusion.34
  17.2 0.6 convolution_add_fusion.1
  17.8 0.8 %fusion.24 = bf16[512,384]{1,0:T(8,128)(2,1)S(1)} fusion(f32[512,384]{1,0:T(8,128)S(1)} %convolution_add_fusion.1, bf16[520,768]{1,0:T(8,128)(2,1)S(1)} %fusion.2, bf16[512,384]{1,0:T(8,128)(2,1)S(1)} %convolution_convert_fusion, bf16[3,768,384]{2,1,0:T(8,128)(2,1)S(1)} %copy-done.2), kind=kOutput, calls=%fused_computation.43 | convolution fusion | flops 304349184 | bytes 2949120 | tf_op jit(solution)/shard_map/dot_general | solution.py:89
  18.6 0.6 slice.172
  19.2 0.6 slice.173
  19.8 2.1 %all_gather.16 = bf16[256,768]{1,0:T(8,128)(2,1)S(1)} all-gather(bf16[256,384]{1,0:T(8,128)(2,1)S(1)} %max.3), channel_id=1, replica_groups=mesh['groups'=2,'seq'=4,'section'=2,'chan'=2] {'chan'}, dimensions={1}, use_global_device_ids=true | all-gather | bytes 589824 | tf_op jit(solution)/shard_map/all_gather | solution.py:99
  21.9 1.4 %convert_reduce_fusion = (f32[4,768]{1,0:T(4,128)S(1)}, bf16[256,768]{1,0:T(8,128)(2,1)}) fusion(bf16[256,768]{1,0:T(8,128)(2,1)S(1)} %all_gather.16, bf16[768,768]{1,0:T(8,128)(2,1)S(1)} %copy-done), kind=kOutput, calls=%fused_computation.56 | convolution fusion | flops 304149504 | bytes 1978368 | tf_op jit(solution)/shard_map/dot_general | solution.py:98
  23.3 1.8 %all_gather.17 = bf16[4,1536]{1,0:T(4,128)(2,1)S(1)} all-gather(bf16[4,768]{1,0:T(4,128)(2,1)S(1)} %multiply_convert_fusion), channel_id=1, replica_groups=mesh['groups'=2,'seq'=4,'section'=2,'chan'=2] {'chan'}, dimensions={1}, use_global_device_ids=true | all-gather | bytes 18432 | tf_op jit(solution)/shard_map/all_gather | solution.py:108
  25.1 0.1 fusion.87
  25.3 0.2 fusion.15
  25.5 26.6 %all-gather = bf16[8,4,256]{2,1,0:T(4,128)(2,1)S(1)} all-gather(bf16[1,4,256]{2,1,0:T(4,128)(2,1)S(1)} %fusion.15), channel_id=1, replica_groups=mesh['groups'=2,'seq'=4,'section'=2,'chan'=2] {'seq','section'}, dimensions={0}, use_global_device_ids=true | all-gather | bytes 18432 | tf_op jit(solution)/shard_map/all_gather | solution.py:121
  52.2 0.1 convert_bitcast_fusion
  52.3 0.1 add_convert_fusion
  52.4 0.1 fusion.85
  52.5 0.1 convolution_add_fusion.11
  52.7 0.1 convolution_add_fusion.10
  52.8 0.1 convolution_add_fusion.9
  53.0 0.1 convolution_add_fusion.8
  53.1 0.1 convolution_add_fusion.7
  53.2 0.1 convolution_add_fusion.6
  53.4 0.1 convolution_add_fusion.5
  53.6 0.1 fusion.13
  53.7 0.1 copy.17
  53.8 2.0 %all_gather.19 = bf16[128,8,16]{2,1,0:T(8,128)(2,1)S(1)} all-gather(bf16[64,8,16]{2,1,0:T(8,128)(2,1)S(1)} %copy.17), channel_id=1, replica_groups=mesh['groups'=2,'seq'=4,'section'=2,'chan'=2] {'chan'}, dimensions={0}, use_global_device_ids=true | all-gather | bytes 49152 | tf_op jit(solution)/shard_map/all_gather | solution.py:141
  55.8 0.2 copy.18
  56.1 2.2 %collective-permute-start.2 = (bf16[128,1,16]{0,2,1:T(8,128)(2,1)S(1)}, bf16[128,1,16]{0,2,1:T(8,128)(2,1)S(1)}, u32[]{:S(2)}, u32[]{:S(2)}) collective-permute-start(bf16[128,1,16]{0,2,1:T(8,128)(2,1)S(1)} %get-tuple-element.10), channel_id=1, source_target_pairs={{0,4},{4,8},{8,12},{1,5},{5,9},{9,13},{2,6},{6,10},{10,14},{3,7},{... | collective-permute-start | bytes 12296 | tf_op jit(solution)/shard_map/ppermute | solution.py:22
  58.3 1.3 %collective-permute-start.3 = (bf16[128,1,16]{0,2,1:T(8,128)(2,1)S(1)}, bf16[128,1,16]{0,2,1:T(8,128)(2,1)S(1)}, u32[]{:S(2)}, u32[]{:S(2)}) collective-permute-start(bf16[128,1,16]{0,2,1:T(8,128)(2,1)S(1)} %get-tuple-element.11), channel_id=1, source_target_pairs={{4,0},{8,4},{12,8},{5,1},{9,5},{13,9},{6,2},{10,6},{14,10},{7,3},{... | collective-permute-start | bytes 12296 | tf_op jit(solution)/shard_map/ppermute | solution.py:24
  59.6 0.1 fusion.94
  59.7 4.0 %collective-permute-done.3 = bf16[128,1,16]{0,2,1:T(8,128)(2,1)S(1)} collective-permute-done((bf16[128,1,16]{0,2,1:T(8,128)(2,1)S(1)}, bf16[128,1,16]{0,2,1:T(8,128)(2,1)S(1)}, u32[]{:S(2)}, u32[]{:S(2)}) %collective-permute-start.3) | collective-permute-done | bytes 4128 | tf_op jit(solution)/shard_map/ppermute | solution.py:24
  63.8 3.0 %collective-permute-start.4 = (bf16[128,10,1]{0,2,1:T(2,128)(2,1)S(1)}, bf16[128,10,1]{0,2,1:T(2,128)(2,1)S(1)}, u32[]{:S(2)}, u32[]{:S(2)}) collective-permute-start(bf16[128,10,1]{0,2,1:T(2,128)(2,1)S(1)} %get-tuple-element.8), channel_id=1, source_target_pairs={{0,2},{1,3},{4,6},{5,7},{8,10},{9,11},{12,14},{13,15},{16,18},{17,... | collective-permute-start | bytes 7688 | tf_op jit(solution)/shard_map/ppermute | solution.py:22
  66.8 1.3 %collective-permute-start.5 = (bf16[128,10,1]{0,2,1:T(2,128)(2,1)S(1)}, bf16[128,10,1]{0,2,1:T(2,128)(2,1)S(1)}, u32[]{:S(2)}, u32[]{:S(2)}) collective-permute-start(bf16[128,10,1]{0,2,1:T(2,128)(2,1)S(1)} %get-tuple-element.9), channel_id=1, source_target_pairs={{2,0},{3,1},{6,4},{7,5},{10,8},{11,9},{14,12},{15,13},{18,16},{19,... | collective-permute-start | bytes 7688 | tf_op jit(solution)/shard_map/ppermute | solution.py:24
  68.1 0.1 fusion.59
  68.2 0.1 fusion.63
  68.4 4.0 %collective-permute-done.5 = bf16[128,10,1]{0,2,1:T(2,128)(2,1)S(1)} collective-permute-done((bf16[128,10,1]{0,2,1:T(2,128)(2,1)S(1)}, bf16[128,10,1]{0,2,1:T(2,128)(2,1)S(1)}, u32[]{:S(2)}, u32[]{:S(2)}) %collective-permute-start.5) | collective-permute-done | bytes 2592 | tf_op jit(solution)/shard_map/ppermute | solution.py:24
  72.4 0.1 fusion.74
  72.5 0.1 fusion.67
  72.6 0.1 fusion.72
  72.8 0.1 fusion.69
  72.9 0.2 fusion.9
  73.1 0.8 %fusion.14 = bf16[64,8,16]{0,2,1:T(8,128)(2,1)} fusion(f32[8,16,64]{2,1,0:T(8,128)S(1)} %fusion.67, f32[8,16,64]{2,1,0:T(8,128)S(1)} %fusion.63, f32[8,16,64]{2,1,0:T(8,128)S(1)} %fusion.69, f32[8,16,64]{2,1,0:T(8,128)S(1)} %fusion.9, bf16[64,8,16]{0,2,1:T(8,128)(2,1)S(1)} %fusion.13, bf16[128,10,17]{0,2,1:T(8,128)(2,1)S(1)} %get-tuple-element.7, ...), kind=kOutput, calls=%fused_computation.31 | convolution fusion | flops 2154496 | bytes 360448 | tf_op jit(solution)/shard_map/co,crs->ors/dot_general | solution.py:43
  (42 shorter events, 0.7 us)
Async XLA Ops:
  0.6 21.3 %copy-start = (bf16[768,768]{1,0:T(8,128)(2,1)S(1)}, bf16[768,768]{1,0:T(8,128)(2,1)}, u32[]{:S(2)}) copy-start(bf16[768,768]{1,0:T(8,128)(2,1)} %param.14) | copy-start | bytes 3538948
  1.7 14.5 %copy-start.6 = (f32[768]{0:T(1024)S(1)}, f32[768]{0:T(1024)}, u32[]{:S(2)}) copy-start(f32[768]{0:T(1024)} %param.12) | copy-start | bytes 9220
  5.6 6.3 %collective-permute-start = (bf16[4,768]{1,0:T(4,128)(2,1)S(1)}, bf16[4,768]{1,0:T(4,128)(2,1)S(1)}, u32[]{:S(2)}, u32[]{:S(2)}) collective-permute-start(bf16[4,768]{1,0:T(4,128)(2,1)S(1)} %get-tuple-element.4), channel_id=1, source_target_pairs={{0,2},{2,4},{4,6},{6,8},{8,10},{10,12},{12,14},{1,3},{3,5},{5,7},{... | collective-permute-start | bytes 18440 | tf_op jit(solution)/shard_map/ppermute | solution.py:22
  10.4 5.5 %collective-permute-start.1 = (bf16[4,768]{1,0:T(4,128)(2,1)S(1)}, bf16[4,768]{1,0:T(4,128)(2,1)S(1)}, u32[]{:S(2)}, u32[]{:S(2)}) collective-permute-start(bf16[4,768]{1,0:T(4,128)(2,1)S(1)} %get-tuple-element.5), channel_id=1, source_target_pairs={{2,0},{4,2},{6,4},{8,6},{10,8},{12,10},{14,12},{3,1},{5,3},{7,5},{... | collective-permute-start | bytes 18440 | tf_op jit(solution)/shard_map/ppermute | solution.py:24
  11.9 4.7 %copy-start.2 = (bf16[3,768,384]{2,1,0:T(8,128)(2,1)S(1)}, bf16[3,768,384]{2,1,0:T(8,128)(2,1)}, u32[]{:S(2)}) copy-start(bf16[3,768,384]{2,1,0:T(8,128)(2,1)} %param.13) | copy-start | bytes 5308420
  21.9 3.3 %copy-start.1 = (bf16[1536,256]{1,0:T(8,128)(2,1)S(1)}, bf16[1536,256]{1,0:T(8,128)(2,1)}, u32[]{:S(2)}) copy-start(bf16[1536,256]{1,0:T(8,128)(2,1)} %param.16) | copy-start | bytes 2359300
  21.9 3.4 %copy-start.5 = (f32[1536]{0:T(1024)S(1)}, f32[1536]{0:T(1024)}, u32[]{:S(2)}) copy-start(f32[1536]{0:T(1024)} %param.15) | copy-start | bytes 18436
  21.9 30.3 %copy-start.7 = (f32[128]{0:T(128)S(1)}, f32[128]{0:T(128)}, u32[]{:S(2)}) copy-start(f32[128]{0:T(128)} %param.17) | copy-start | bytes 1540
  21.9 30.5 %copy-start.3 = (bf16[3,3,128,64]{2,3,1,0:T(8,128)(2,1)S(1)}, bf16[3,3,128,64]{2,3,1,0:T(8,128)(2,1)}, u32[]{:S(2)}) copy-start(bf16[3,3,128,64]{2,3,1,0:T(8,128)(2,1)} %param.18) | copy-start | bytes 442372
  25.5 34.0 %copy-start.4 = (bf16[3,3,128,64]{2,3,1,0:T(8,128)(2,1)S(1)}, bf16[3,3,128,64]{2,3,1,0:T(8,128)(2,1)}, u32[]{:S(2)}) copy-start(bf16[3,3,128,64]{2,3,1,0:T(8,128)(2,1)} %param.19) | copy-start | bytes 442372
  56.1 3.6 %collective-permute-start.2 = (bf16[128,1,16]{0,2,1:T(8,128)(2,1)S(1)}, bf16[128,1,16]{0,2,1:T(8,128)(2,1)S(1)}, u32[]{:S(2)}, u32[]{:S(2)}) collective-permute-start(bf16[128,1,16]{0,2,1:T(8,128)(2,1)S(1)} %get-tuple-element.10), channel_id=1, source_target_pairs={{0,4},{4,8},{8,12},{1,5},{5,9},{9,13},{2,6},{6,10},{10,14},{3,7},{... | collective-permute-start | bytes 12296 | tf_op jit(solution)/shard_map/ppermute | solution.py:22
  58.3 5.5 %collective-permute-start.3 = (bf16[128,1,16]{0,2,1:T(8,128)(2,1)S(1)}, bf16[128,1,16]{0,2,1:T(8,128)(2,1)S(1)}, u32[]{:S(2)}, u32[]{:S(2)}) collective-permute-start(bf16[128,1,16]{0,2,1:T(8,128)(2,1)S(1)} %get-tuple-element.11), channel_id=1, source_target_pairs={{4,0},{8,4},{12,8},{5,1},{9,5},{13,9},{6,2},{10,6},{14,10},{7,3},{... | collective-permute-start | bytes 12296 | tf_op jit(solution)/shard_map/ppermute | solution.py:24
  63.8 4.6 %collective-permute-start.4 = (bf16[128,10,1]{0,2,1:T(2,128)(2,1)S(1)}, bf16[128,10,1]{0,2,1:T(2,128)(2,1)S(1)}, u32[]{:S(2)}, u32[]{:S(2)}) collective-permute-start(bf16[128,10,1]{0,2,1:T(2,128)(2,1)S(1)} %get-tuple-element.8), channel_id=1, source_target_pairs={{0,2},{1,3},{4,6},{5,7},{8,10},{9,11},{12,14},{13,15},{16,18},{17,... | collective-permute-start | bytes 7688 | tf_op jit(solution)/shard_map/ppermute | solution.py:22
  66.8 5.5 %collective-permute-start.5 = (bf16[128,10,1]{0,2,1:T(2,128)(2,1)S(1)}, bf16[128,10,1]{0,2,1:T(2,128)(2,1)S(1)}, u32[]{:S(2)}, u32[]{:S(2)}) collective-permute-start(bf16[128,10,1]{0,2,1:T(2,128)(2,1)S(1)} %get-tuple-element.9), channel_id=1, source_target_pairs={{2,0},{3,1},{6,4},{7,5},{10,8},{11,9},{14,12},{15,13},{18,16},{19,... | collective-permute-start | bytes 7688 | tf_op jit(solution)/shard_map/ppermute | solution.py:24
where the time goes:
time: 74.2 us; the launch traced here: 73.8 us
  blocking collectives  35 us (47%)
  starting transfers between devices  13.8 us (19%)
  waiting for transfers between devices  12 us (16%)
  matrix products  7.84 us (11%)
  local copies, waits for them, and re-layouts  2.83 us (4%)
  other arithmetic  1.39 us (2%)
  between operations  0.97 us (1%)
    all_gather x1, blocking collectives, per_device(): lax.all_gather(factors, ('seq', 'section'), axis=0, tiled=True)  26.6 us
    ppermute x3, waiting for transfers between devices, padded(): lax.ppermute(head, axis, [((i + 1) % count, i) for i in range(ends)])  12 us
    ppermute x3, starting transfers between devices, padded(): lax.ppermute(tail, axis, [(i, (i + 1) % count) for i in range(ends)])  9.96 us
    ppermute x3, starting transfers between devices, padded(): lax.ppermute(head, axis, [((i + 1) % count, i) for i in range(ends)])  3.88 us
    dot_general x18, matrix products, pair_conv(): jnp.einsum('co,crs->ors', weight[shift_row, shift_col], window, preferred...  3.11 us
    all_gather x1, blocking collectives, per_device(): full_stem_output = lax.all_gather(stem_own, 'chan', axis=1, tiled=True)  2.49 us
    all_gather x1, blocking collectives, per_device(): lax.all_gather(halved, 'chan', axis=1, tiled=True)  2.09 us
    all_gather x1, blocking collectives, per_device(): mid_full = lax.all_gather(pair_mid, 'chan', axis=0, tiled=True)  1.99 us
  transfers between devices with their start and end apart: 6, of which 3 were waited for; matrix products, arithmetic and copies ran while one was open for 1% of the time, Pallas kernels for 0%

commit v1 on v0

--- a/solution.py
+++ b/solution.py
@@ -3,6 +3,7 @@
 import jax.numpy as jnp
 from jax import lax
 from jax.sharding import PartitionSpec as P
+from jax.lax import axis_index, axis_size, ppermute
 
 PC = 128
 PATCH = 16
@@ -118,7 +119,23 @@
     row_anchor = lax.axis_index("seq") * tile_height
     col_anchor = lax.axis_index("section") * tile_width
     pair_own = pair_weight_one.shape[3]
-    every_token = lax.all_gather(factors, ("seq", "section"), axis=0, tiled=True)
+    wide_out, odd, p_next = (
+        axis_size(("seq", "section")),
+        axis_index(("seq", "section")),
+        factors.shape[0],
+    )
+    placed, n_now = (factors, 1)
+    while n_now < wide_out:
+        series = []
+        at = 0
+        while at < wide_out:
+            series.append((at, (at - n_now) % wide_out))
+            at = at + 1
+        placed = jnp.concatenate(
+            [placed, ppermute(placed, axis_name=("seq", "section"), perm=series)], axis=0
+        )
+        n_now = 2 * n_now
+    every_token = jnp.roll(placed, odd * p_next, axis=0)
     zero_padded = jnp.pad(every_token, ((1, 1), (0, 0)))
     row_factor = lax.dynamic_slice_in_dim(zero_padded, row_anchor, tile_height + 2, 0)[:, :PC]
     col_factor = lax.dynamic_slice_in_dim(zero_padded, col_anchor, tile_width + 2, 0)[:, PC:]

time: 74.2 us -> 63.6 us (0.86)
  blocking collectives: 35 us -> 8.39 us
  starting transfers between devices: 13.8 us -> 24.3 us
  waiting for transfers between devices: 12 us -> 17.5 us
    all_gather x1 -> x0, blocking collectives: 26.6 us -> none  [per_device(): lax.all_gather(factors, ('seq', 'section'), axis=0, tiled=True)]
    ppermute x0 -> x3, starting transfers between devices: none -> 7.7 us  [per_device(): ppermute(placed, axis_name=('seq', 'section'), perm=series)]
    ppermute x0 -> x3, waiting for transfers between devices: none -> 5.37 us  [per_device(): ppermute(placed, axis_name=('seq', 'section'), perm=series)]
    ppermute x3, starting transfers between devices: 9.96 us -> 12.8 us  [padded(): lax.ppermute(tail, axis, [(i, (i + 1) % count) for i in range(ends)])]
  transfers between devices with their start and end apart: 6 -> 9, of which waited for: 3 -> 6; matrix products, arithmetic and copies ran while one was open for 1% -> 1% of each run, Pallas kernels for 0% -> 0%
where the time goes in v1:
time: 63.6 us; the launch traced here: 63.3 us
  starting transfers between devices  24.3 us (38%)
  waiting for transfers between devices  17.5 us (28%)
  blocking collectives  8.39 us (13%)
  matrix products  7.84 us (12%)
  local copies, waits for them, and re-layouts  2.89 us (5%)
  other arithmetic  1.4 us (2%)
  between operations  0.98 us (2%)
    ppermute x3, starting transfers between devices, padded(): lax.ppermute(tail, axis, [(i, (i + 1) % count) for i in range(ends)])  12.8 us
    ppermute x3, waiting for transfers between devices, padded(): lax.ppermute(head, axis, [((i + 1) % count, i) for i in range(ends)])  12.1 us
    ppermute x3, starting transfers between devices, per_device(): ppermute(placed, axis_name=('seq', 'section'), perm=series)  7.7 us
    ppermute x3, waiting for transfers between devices, per_device(): ppermute(placed, axis_name=('seq', 'section'), perm=series)  5.37 us
    ppermute x3, starting transfers between devices, padded(): lax.ppermute(head, axis, [((i + 1) % count, i) for i in range(ends)])  3.88 us
    dot_general x18, matrix products, pair_conv(): jnp.einsum('co,crs->ors', weight[shift_row, shift_col], window, preferred...  3.11 us
    all_gather x1, blocking collectives, per_device(): full_stem_output = lax.all_gather(stem_own, 'chan', axis=1, tiled=True)  2.49 us
    all_gather x1, blocking collectives, per_device(): lax.all_gather(halved, 'chan', axis=1, tiled=True)  2.09 us
  transfers between devices with their start and end apart: 9, of which 6 were waited for; matrix products, arithmetic and copies ran while one was open for 1% of the time, Pallas kernels for 0%

profile of v1, /device:TPU:0, one launch (start us, length us, event | category | flops | bytes accessed | tf_op | source)
XLA Modules:
  0.0 63.3 jit_solution(9614648014909008688)
XLA Ops:
  0.7 1.0 %eq.25 = s32[512,16]{1,0:T(8,128)S(1)} reshape(s32[8192]{0:T(1024)} %param.10) | data formatting | bytes 65536 | tf_op jit(solution)/shard_map/eq | solution.py:77
  1.9 1.2 %convolution_convert_fusion = bf16[512,384]{1,0:T(8,128)(2,1)S(1)} fusion(s32[512,64]{0,1:T(8,128)S(1)} %eq.27, s32[64]{0:T(128)S(1)} %eq.29, bf16[64,768]{1,0:T(8,128)(2,1)} %param.11, s32[]{:T(128)S(6)} %select_n.29), kind=kOutput, calls=%fused_computation.7 | convolution fusion | flops 25395200 | bytes 573700 | tf_op jit(solution)/shard_map/dot_general | solution.py:84
  3.1 2.5 %all_gather.12 = bf16[512,768]{1,0:T(8,128)(2,1)S(1)} all-gather(bf16[512,384]{1,0:T(8,128)(2,1)S(1)} %convolution_convert_fusion), channel_id=1, replica_groups=mesh['groups'=2,'seq'=4,'section'=2,'chan'=2] {'chan'}, dimensions={1}, use_global_device_ids=true | all-gather | bytes 1179648 | tf_op jit(solution)/shard_map/all_gather | solution.py:85
  5.6 4.8 %collective-permute-start = (bf16[4,768]{1,0:T(4,128)(2,1)S(1)}, bf16[4,768]{1,0:T(4,128)(2,1)S(1)}, u32[]{:S(2)}, u32[]{:S(2)}) collective-permute-start(bf16[4,768]{1,0:T(4,128)(2,1)S(1)} %get-tuple-element.4), channel_id=1, source_target_pairs={{0,2},{2,4},{4,6},{6,8},{8,10},{10,12},{12,14},{1,3},{3,5},{5,7},{... | collective-permute-start | bytes 18440 | tf_op jit(solution)/shard_map/ppermute | solution.py:23
  10.4 1.3 %collective-permute-start.1 = (bf16[4,768]{1,0:T(4,128)(2,1)S(1)}, bf16[4,768]{1,0:T(4,128)(2,1)S(1)}, u32[]{:S(2)}, u32[]{:S(2)}) collective-permute-start(bf16[4,768]{1,0:T(4,128)(2,1)S(1)} %get-tuple-element.5), channel_id=1, source_target_pairs={{2,0},{4,2},{6,4},{8,6},{10,8},{12,10},{14,12},{3,1},{5,3},{7,5},{... | collective-permute-start | bytes 18440 | tf_op jit(solution)/shard_map/ppermute | solution.py:25
  11.8 4.1 %collective-permute-done.1 = bf16[4,768]{1,0:T(4,128)(2,1)S(1)} collective-permute-done((bf16[4,768]{1,0:T(4,128)(2,1)S(1)}, bf16[4,768]{1,0:T(4,128)(2,1)S(1)}, u32[]{:S(2)}, u32[]{:S(2)}) %collective-permute-start.1) | collective-permute-done | bytes 6176 | tf_op jit(solution)/shard_map/ppermute | solution.py:25
  15.9 0.3 fusion
  16.3 0.3 fusion.2
  16.6 0.6 fusion.33
  17.2 0.6 convolution_add_fusion.1
  17.8 0.8 %fusion.23 = bf16[512,384]{1,0:T(8,128)(2,1)S(1)} fusion(f32[512,384]{1,0:T(8,128)S(1)} %convolution_add_fusion.1, bf16[520,768]{1,0:T(8,128)(2,1)S(1)} %fusion.2, bf16[512,384]{1,0:T(8,128)(2,1)S(1)} %convolution_convert_fusion, bf16[3,768,384]{2,1,0:T(8,128)(2,1)S(1)} %copy-done.2), kind=kOutput, calls=%fused_computation.42 | convolution fusion | flops 304349184 | bytes 2949120 | tf_op jit(solution)/shard_map/dot_general | solution.py:90
  18.6 0.6 slice.172
  19.2 0.6 slice.173
  19.8 2.1 %all_gather.13 = bf16[256,768]{1,0:T(8,128)(2,1)S(1)} all-gather(bf16[256,384]{1,0:T(8,128)(2,1)S(1)} %max.3), channel_id=1, replica_groups=mesh['groups'=2,'seq'=4,'section'=2,'chan'=2] {'chan'}, dimensions={1}, use_global_device_ids=true | all-gather | bytes 589824 | tf_op jit(solution)/shard_map/all_gather | solution.py:100
  21.9 1.4 %convert_reduce_fusion = (f32[4,768]{1,0:T(4,128)S(1)}, bf16[256,768]{1,0:T(8,128)(2,1)}) fusion(bf16[256,768]{1,0:T(8,128)(2,1)S(1)} %all_gather.13, bf16[768,768]{1,0:T(8,128)(2,1)S(1)} %copy-done), kind=kOutput, calls=%fused_computation.55 | convolution fusion | flops 304149504 | bytes 1978368 | tf_op jit(solution)/shard_map/dot_general | solution.py:99
  23.3 1.8 %all_gather.14 = bf16[4,1536]{1,0:T(4,128)(2,1)S(1)} all-gather(bf16[4,768]{1,0:T(4,128)(2,1)S(1)} %multiply_convert_fusion), channel_id=1, replica_groups=mesh['groups'=2,'seq'=4,'section'=2,'chan'=2] {'chan'}, dimensions={1}, use_global_device_ids=true | all-gather | bytes 18432 | tf_op jit(solution)/shard_map/all_gather | solution.py:109
  25.3 0.2 convolution_convert_fusion.1
  25.5 2.8 %collective-permute-start.2 = (bf16[4,256]{1,0:T(4,128)(2,1)S(1)}, bf16[4,256]{1,0:T(4,128)(2,1)S(1)}, u32[]{:S(2)}, u32[]{:S(2)}) collective-permute-start(bf16[4,256]{1,0:T(4,128)(2,1)S(1)} %convolution_convert_fusion.1), channel_id=1, source_target_pairs={{0,14},{2,0},{4,2},{6,4},{8,6},{10,8},{12,10},{14,12},{1,15},{3,1}... | collective-permute-start | bytes 6152 | tf_op jit(solution)/shard_map/ppermute | solution.py:135
  28.3 1.3 %collective-permute-done.2 = bf16[4,256]{1,0:T(4,128)(2,1)S(1)} collective-permute-done((bf16[4,256]{1,0:T(4,128)(2,1)S(1)}, bf16[4,256]{1,0:T(4,128)(2,1)S(1)}, u32[]{:S(2)}, u32[]{:S(2)}) %collective-permute-start.2) | collective-permute-done | bytes 2080 | tf_op jit(solution)/shard_map/ppermute | solution.py:135
  29.6 3.2 %collective-permute-start.3 = (bf16[8,256]{1,0:T(8,128)(2,1)S(1)}, bf16[8,256]{1,0:T(8,128)(2,1)S(1)}, u32[]{:S(2)}, u32[]{:S(2)}) collective-permute-start(bf16[8,256]{1,0:T(8,128)(2,1)S(1)} %pad_maximum_fusion.6), channel_id=1, source_target_pairs={{0,12},{2,14},{4,0},{6,2},{8,4},{10,6},{12,8},{14,10},{1,13},{3,15... | collective-permute-start | bytes 12296 | tf_op jit(solution)/shard_map/ppermute | solution.py:135
  32.8 1.3 %collective-permute-done.3 = bf16[8,256]{1,0:T(8,128)(2,1)S(1)} collective-permute-done((bf16[8,256]{1,0:T(8,128)(2,1)S(1)}, bf16[8,256]{1,0:T(8,128)(2,1)S(1)}, u32[]{:S(2)}, u32[]{:S(2)}) %collective-permute-start.3) | collective-permute-done | bytes 4128 | tf_op jit(solution)/shard_map/ppermute | solution.py:135
  34.2 1.7 %collective-permute-start.4 = (bf16[16,256]{1,0:T(8,128)(2,1)S(1)}, bf16[16,256]{1,0:T(8,128)(2,1)S(1)}, u32[]{:S(2)}, u32[]{:S(2)}) collective-permute-start(bf16[16,256]{1,0:T(8,128)(2,1)S(1)} %pad_maximum_fusion.2), channel_id=1, source_target_pairs={{0,8},{2,10},{4,12},{6,14},{8,0},{10,2},{12,4},{14,6},{1,9},{3,11}... | collective-permute-start | bytes 24584 | tf_op jit(solution)/shard_map/ppermute | solution.py:135
  36.0 2.8 %collective-permute-done.4 = bf16[16,256]{1,0:T(8,128)(2,1)S(1)} collective-permute-done((bf16[16,256]{1,0:T(8,128)(2,1)S(1)}, bf16[16,256]{1,0:T(8,128)(2,1)S(1)}, u32[]{:S(2)}, u32[]{:S(2)}) %collective-permute-start.4) | collective-permute-done | bytes 8224 | tf_op jit(solution)/shard_map/ppermute | solution.py:135
  38.9 0.1 add_convert_fusion
  39.2 0.1 convolution_add_fusion.11
  39.3 0.1 convolution_add_fusion.10
  39.5 0.1 convolution_add_fusion.9
  39.6 0.1 convolution_add_fusion.8
  39.8 0.1 convolution_add_fusion.7
  39.9 0.1 convolution_add_fusion.6
  40.0 0.1 convolution_add_fusion.5
  40.2 0.1 fusion.13
  40.4 0.1 copy.17
  40.5 2.0 %all_gather.15 = bf16[128,8,16]{2,1,0:T(8,128)(2,1)S(1)} all-gather(bf16[64,8,16]{2,1,0:T(8,128)(2,1)S(1)} %copy.17), channel_id=1, replica_groups=mesh['groups'=2,'seq'=4,'section'=2,'chan'=2] {'chan'}, dimensions={0}, use_global_device_ids=true | all-gather | bytes 49152 | tf_op jit(solution)/shard_map/all_gather | solution.py:158
  42.5 0.2 copy.18
  42.7 3.7 %collective-permute-start.5 = (bf16[128,1,16]{0,2,1:T(8,128)(2,1)S(1)}, bf16[128,1,16]{0,2,1:T(8,128)(2,1)S(1)}, u32[]{:S(2)}, u32[]{:S(2)}) collective-permute-start(bf16[128,1,16]{0,2,1:T(8,128)(2,1)S(1)} %get-tuple-element.10), channel_id=1, source_target_pairs={{0,4},{4,8},{8,12},{1,5},{5,9},{9,13},{2,6},{6,10},{10,14},{3,7},{... | collective-permute-start | bytes 12296 | tf_op jit(solution)/shard_map/ppermute | solution.py:23
  46.4 1.3 %collective-permute-start.6 = (bf16[128,1,16]{0,2,1:T(8,128)(2,1)S(1)}, bf16[128,1,16]{0,2,1:T(8,128)(2,1)S(1)}, u32[]{:S(2)}, u32[]{:S(2)}) collective-permute-start(bf16[128,1,16]{0,2,1:T(8,128)(2,1)S(1)} %get-tuple-element.11), channel_id=1, source_target_pairs={{4,0},{8,4},{12,8},{5,1},{9,5},{13,9},{6,2},{10,6},{14,10},{7,3},{... | collective-permute-start | bytes 12296 | tf_op jit(solution)/shard_map/ppermute | solution.py:25
  47.7 0.1 fusion.93
  47.9 4.0 %collective-permute-done.6 = bf16[128,1,16]{0,2,1:T(8,128)(2,1)S(1)} collective-permute-done((bf16[128,1,16]{0,2,1:T(8,128)(2,1)S(1)}, bf16[128,1,16]{0,2,1:T(8,128)(2,1)S(1)}, u32[]{:S(2)}, u32[]{:S(2)}) %collective-permute-start.6) | collective-permute-done | bytes 4128 | tf_op jit(solution)/shard_map/ppermute | solution.py:25
  51.9 4.3 %collective-permute-start.7 = (bf16[128,10,1]{0,2,1:T(2,128)(2,1)S(1)}, bf16[128,10,1]{0,2,1:T(2,128)(2,1)S(1)}, u32[]{:S(2)}, u32[]{:S(2)}) collective-permute-start(bf16[128,10,1]{0,2,1:T(2,128)(2,1)S(1)} %get-tuple-element.8), channel_id=1, source_target_pairs={{0,2},{1,3},{4,6},{5,7},{8,10},{9,11},{12,14},{13,15},{16,18},{17,... | collective-permute-start | bytes 7688 | tf_op jit(solution)/shard_map/ppermute | solution.py:23
  56.3 1.3 %collective-permute-start.8 = (bf16[128,10,1]{0,2,1:T(2,128)(2,1)S(1)}, bf16[128,10,1]{0,2,1:T(2,128)(2,1)S(1)}, u32[]{:S(2)}, u32[]{:S(2)}) collective-permute-start(bf16[128,10,1]{0,2,1:T(2,128)(2,1)S(1)} %get-tuple-element.9), channel_id=1, source_target_pairs={{2,0},{3,1},{6,4},{7,5},{10,8},{11,9},{14,12},{15,13},{18,16},{19,... | collective-permute-start | bytes 7688 | tf_op jit(solution)/shard_map/ppermute | solution.py:25
  57.7 0.1 fusion.62
  57.8 4.0 %collective-permute-done.8 = bf16[128,10,1]{0,2,1:T(2,128)(2,1)S(1)} collective-permute-done((bf16[128,10,1]{0,2,1:T(2,128)(2,1)S(1)}, bf16[128,10,1]{0,2,1:T(2,128)(2,1)S(1)}, u32[]{:S(2)}, u32[]{:S(2)}) %collective-permute-start.8) | collective-permute-done | bytes 2592 | tf_op jit(solution)/shard_map/ppermute | solution.py:25
  61.9 0.1 fusion.66
  62.1 0.1 fusion.71
  62.2 0.1 fusion.68
  62.3 0.2 fusion.9
  62.5 0.8 %fusion.14 = bf16[64,8,16]{0,2,1:T(8,128)(2,1)} fusion(f32[8,16,64]{2,1,0:T(8,128)S(1)} %fusion.66, f32[8,16,64]{2,1,0:T(8,128)S(1)} %fusion.62, f32[8,16,64]{2,1,0:T(8,128)S(1)} %fusion.68, f32[8,16,64]{2,1,0:T(8,128)S(1)} %fusion.9, bf16[64,8,16]{0,2,1:T(8,128)(2,1)S(1)} %fusion.13, bf16[128,10,17]{0,2,1:T(8,128)(2,1)S(1)} %get-tuple-element.7, ...), kind=kOutput, calls=%fused_computation.31 | convolution fusion | flops 2154496 | bytes 360448 | tf_op jit(solution)/shard_map/co,crs->ors/dot_general | solution.py:44
  (50 shorter events, 1.4 us)
Async XLA Ops:
  0.6 21.3 %copy-start = (bf16[768,768]{1,0:T(8,128)(2,1)S(1)}, bf16[768,768]{1,0:T(8,128)(2,1)}, u32[]{:S(2)}) copy-start(bf16[768,768]{1,0:T(8,128)(2,1)} %param.14) | copy-start | bytes 3538948
  1.7 14.5 %copy-start.6 = (f32[768]{0:T(1024)S(1)}, f32[768]{0:T(1024)}, u32[]{:S(2)}) copy-start(f32[768]{0:T(1024)} %param.12) | copy-start | bytes 9220
  5.6 6.2 %collective-permute-start = (bf16[4,768]{1,0:T(4,128)(2,1)S(1)}, bf16[4,768]{1,0:T(4,128)(2,1)S(1)}, u32[]{:S(2)}, u32[]{:S(2)}) collective-permute-start(bf16[4,768]{1,0:T(4,128)(2,1)S(1)} %get-tuple-element.4), channel_id=1, source_target_pairs={{0,2},{2,4},{4,6},{6,8},{8,10},{10,12},{12,14},{1,3},{3,5},{5,7},{... | collective-permute-start | bytes 18440 | tf_op jit(solution)/shard_map/ppermute | solution.py:23
  10.4 5.5 %collective-permute-start.1 = (bf16[4,768]{1,0:T(4,128)(2,1)S(1)}, bf16[4,768]{1,0:T(4,128)(2,1)S(1)}, u32[]{:S(2)}, u32[]{:S(2)}) collective-permute-start(bf16[4,768]{1,0:T(4,128)(2,1)S(1)} %get-tuple-element.5), channel_id=1, source_target_pairs={{2,0},{4,2},{6,4},{8,6},{10,8},{12,10},{14,12},{3,1},{5,3},{7,5},{... | collective-permute-start | bytes 18440 | tf_op jit(solution)/shard_map/ppermute | solution.py:25
  11.7 4.9 %copy-start.2 = (bf16[3,768,384]{2,1,0:T(8,128)(2,1)S(1)}, bf16[3,768,384]{2,1,0:T(8,128)(2,1)}, u32[]{:S(2)}) copy-start(bf16[3,768,384]{2,1,0:T(8,128)(2,1)} %param.13) | copy-start | bytes 5308420
  21.9 3.3 %copy-start.1 = (bf16[1536,256]{1,0:T(8,128)(2,1)S(1)}, bf16[1536,256]{1,0:T(8,128)(2,1)}, u32[]{:S(2)}) copy-start(bf16[1536,256]{1,0:T(8,128)(2,1)} %param.16) | copy-start | bytes 2359300
  21.9 3.4 %copy-start.5 = (f32[1536]{0:T(1024)S(1)}, f32[1536]{0:T(1024)}, u32[]{:S(2)}) copy-start(f32[1536]{0:T(1024)} %param.15) | copy-start | bytes 18436
  21.9 17.0 %copy-start.7 = (f32[128]{0:T(128)S(1)}, f32[128]{0:T(128)}, u32[]{:S(2)}) copy-start(f32[128]{0:T(128)} %param.17) | copy-start | bytes 1540
  21.9 17.1 %copy-start.3 = (bf16[3,3,128,64]{2,3,1,0:T(8,128)(2,1)S(1)}, bf16[3,3,128,64]{2,3,1,0:T(8,128)(2,1)}, u32[]{:S(2)}) copy-start(bf16[3,3,128,64]{2,3,1,0:T(8,128)(2,1)} %param.18) | copy-start | bytes 442372
  25.5 22.2 %copy-start.4 = (bf16[3,3,128,64]{2,3,1,0:T(8,128)(2,1)S(1)}, bf16[3,3,128,64]{2,3,1,0:T(8,128)(2,1)}, u32[]{:S(2)}) copy-start(bf16[3,3,128,64]{2,3,1,0:T(8,128)(2,1)} %param.19) | copy-start | bytes 442372
  25.5 4.1 %collective-permute-start.2 = (bf16[4,256]{1,0:T(4,128)(2,1)S(1)}, bf16[4,256]{1,0:T(4,128)(2,1)S(1)}, u32[]{:S(2)}, u32[]{:S(2)}) collective-permute-start(bf16[4,256]{1,0:T(4,128)(2,1)S(1)} %convolution_convert_fusion.1), channel_id=1, source_target_pairs={{0,14},{2,0},{4,2},{6,4},{8,6},{10,8},{12,10},{14,12},{1,15},{3,1}... | collective-permute-start | bytes 6152 | tf_op jit(solution)/shard_map/ppermute | solution.py:135
  29.6 4.5 %collective-permute-start.3 = (bf16[8,256]{1,0:T(8,128)(2,1)S(1)}, bf16[8,256]{1,0:T(8,128)(2,1)S(1)}, u32[]{:S(2)}, u32[]{:S(2)}) collective-permute-start(bf16[8,256]{1,0:T(8,128)(2,1)S(1)} %pad_maximum_fusion.6), channel_id=1, source_target_pairs={{0,12},{2,14},{4,0},{6,2},{8,4},{10,6},{12,8},{14,10},{1,13},{3,15... | collective-permute-start | bytes 12296 | tf_op jit(solution)/shard_map/ppermute | solution.py:135
  34.2 4.5 %collective-permute-start.4 = (bf16[16,256]{1,0:T(8,128)(2,1)S(1)}, bf16[16,256]{1,0:T(8,128)(2,1)S(1)}, u32[]{:S(2)}, u32[]{:S(2)}) collective-permute-start(bf16[16,256]{1,0:T(8,128)(2,1)S(1)} %pad_maximum_fusion.2), channel_id=1, source_target_pairs={{0,8},{2,10},{4,12},{6,14},{8,0},{10,2},{12,4},{14,6},{1,9},{3,11}... | collective-permute-start | bytes 24584 | tf_op jit(solution)/shard_map/ppermute | solution.py:135
  42.7 5.2 %collective-permute-start.5 = (bf16[128,1,16]{0,2,1:T(8,128)(2,1)S(1)}, bf16[128,1,16]{0,2,1:T(8,128)(2,1)S(1)}, u32[]{:S(2)}, u32[]{:S(2)}) collective-permute-start(bf16[128,1,16]{0,2,1:T(8,128)(2,1)S(1)} %get-tuple-element.10), channel_id=1, source_target_pairs={{0,4},{4,8},{8,12},{1,5},{5,9},{9,13},{2,6},{6,10},{10,14},{3,7},{... | collective-permute-start | bytes 12296 | tf_op jit(solution)/shard_map/ppermute | solution.py:23
  46.4 5.5 %collective-permute-start.6 = (bf16[128,1,16]{0,2,1:T(8,128)(2,1)S(1)}, bf16[128,1,16]{0,2,1:T(8,128)(2,1)S(1)}, u32[]{:S(2)}, u32[]{:S(2)}) collective-permute-start(bf16[128,1,16]{0,2,1:T(8,128)(2,1)S(1)} %get-tuple-element.11), channel_id=1, source_target_pairs={{4,0},{8,4},{12,8},{5,1},{9,5},{13,9},{6,2},{10,6},{14,10},{7,3},{... | collective-permute-start | bytes 12296 | tf_op jit(solution)/shard_map/ppermute | solution.py:25
  51.9 5.9 %collective-permute-start.7 = (bf16[128,10,1]{0,2,1:T(2,128)(2,1)S(1)}, bf16[128,10,1]{0,2,1:T(2,128)(2,1)S(1)}, u32[]{:S(2)}, u32[]{:S(2)}) collective-permute-start(bf16[128,10,1]{0,2,1:T(2,128)(2,1)S(1)} %get-tuple-element.8), channel_id=1, source_target_pairs={{0,2},{1,3},{4,6},{5,7},{8,10},{9,11},{12,14},{13,15},{16,18},{17,... | collective-permute-start | bytes 7688 | tf_op jit(solution)/shard_map/ppermute | solution.py:23
  56.3 5.5 %collective-permute-start.8 = (bf16[128,10,1]{0,2,1:T(2,128)(2,1)S(1)}, bf16[128,10,1]{0,2,1:T(2,128)(2,1)S(1)}, u32[]{:S(2)}, u32[]{:S(2)}) collective-permute-start(bf16[128,10,1]{0,2,1:T(2,128)(2,1)S(1)} %get-tuple-element.9), channel_id=1, source_target_pairs={{2,0},{3,1},{6,4},{7,5},{10,8},{11,9},{14,12},{15,13},{18,16},{19,... | collective-permute-start | bytes 7688 | tf_op jit(solution)/shard_map/ppermute | solution.py:25
